TPU v7x, 128 devices: a whole 4x4x4 slice. The times are simulated.
128 devices in a mesh: wide: 32 (over x, z, core), narrow: 4 (over y).
Axes of the slice: x: 4, y: 4, z: 4, core: 2. Of those that a mesh axis runs over, the one named last changes fastest.
Arguments:
- member: bfloat16 [2048, 8192], P('narrow', 'wide'), may hold values from 0.01 to 300, as said below
Outputs:
- transition: float32 [8192, 8192], P('wide', 'narrow')
- stationary: float32 [8192], P('wide')
Inputs may be any that keep to these rules, and one draw needn't show every extreme that they name: `member`: strictly positive weights.
All inputs are finite; a program needn't handle non-finite values.
Results may differ from a plain program's by a relative error of at most 0.0003.
Values may be sent and summed in bfloat16 or wider, within the bound.
No kernel may reach another device: no remote copies, remote signals or barrier semaphores. Data moves between devices by JAX's collectives and lax.ppermute only.
A program may use at most 128 MiB of HBM per device.

v0:
```python
import jax
import jax.numpy as jnp
from jax import lax
from jax.sharding import PartitionSpec as P

STATES = 8192
TAU = 64
ITERS = 3


def passed_along(block, axis, distance):
    devices = range(lax.axis_size(axis))
    route = [(i - distance, i) for i in devices if i - distance in devices]
    return lax.ppermute(block, axis, route)


def contract_frames(left, right):
    return lax.dot_general(
        left, right, (((0,), (0,)), ((), ())), preferred_element_type=jnp.float32
    )


def shards(member):
    rim = passed_along(member[:TAU], "narrow", -1)
    lagged = jnp.concatenate([member[TAU:], rim], axis=0)
    frame_part = jnp.sum(lagged, axis=1, dtype=jnp.float32)
    frame_totals = lax.psum(frame_part, "wide")
    visit_part = jnp.dot(frame_totals, member.astype(jnp.float32), precision=lax.Precision.HIGHEST)
    stacked = jnp.stack([member, lagged])
    piece = lax.all_gather(stacked, "wide", axis=2, tiled=True)
    partial_value = contract_frames(member, piece[1]) + contract_frames(lagged, piece[0])
    counts = lax.psum_scatter(partial_value, "narrow", scatter_dimension=1, tiled=True)
    row_now, visit_rows = lax.psum((jnp.sum(counts, axis=1), visit_part), "narrow")
    visit_all = lax.all_gather(visit_rows, "wide", axis=0, tiled=True)
    width_cols = counts.shape[1]
    col_start = lax.axis_index("narrow") * width_cols
    visit_cols = lax.dynamic_slice_in_dim(visit_all, col_start, width_cols)
    estimate = counts
    for step in range(ITERS):
        all_rows = lax.all_gather(row_now, "wide", axis=0, tiled=True)
        col_now = lax.dynamic_slice_in_dim(all_rows, col_start, width_cols)
        ratio_rows = visit_rows / row_now
        ratio_cols = visit_cols / col_now
        estimate = counts / (ratio_rows[:, None] + ratio_cols[None, :])
        row_now = lax.psum(jnp.sum(estimate, axis=1), "narrow")
    transition = STATES * estimate / row_now[:, None]
    grand = lax.psum(jnp.sum(row_now), "wide")
    stationary = STATES * row_now / grand
    return (transition, stationary)


def solution(mesh):
    return jax.shard_map(
        shards,
        mesh=mesh,
        in_specs=(P("narrow", "wide"),),
        out_specs=(P("wide", "narrow"), P("wide")),
        check_vma=False,
    )
```

profile of v0, /device:TPU:1, one launch (start us, length us, event | category | flops | bytes accessed | tf_op | source)
XLA Modules:
  0.0 404.0 jit_solution(7120169739386829088)
XLA Ops:
  7.2 0.0 all-gather.6.cloned.1.call-start
  7.2 0.8 slice.13
  8.0 1.3 collective-permute-start
  9.3 1.0 slice.12
  10.3 3.1 collective-permute-done
  13.3 1.8 pad_maximum_fusion
  15.1 0.0 all-gather.6.cloned.1.call-update
  15.2 0.0 reduce-scatter.2.cloned.1.call-start
  15.2 84.3 %all-gather.6.cloned.1.call-done = bf16[2,512,8192]{2,1,0:T(8,128)(2,1)} async-done(((bf16[2,512,256]{2,1,0:T(8,128)(2,1)}), bf16[2,512,8192]{2,1,0:T(8,128)(2,1)}) %all-gather.6.cloned.1.call-update) | async-done | bytes 16777232 | tf_op jit(solution)/shard_map/all_gather | solution.py:30
  99.5 5.8 %convolution_bitcast_fusion = f32[256,8192]{0,1:T(8,128)S(1)} fusion(bf16[512,256]{1,0:T(8,128)(2,1)S(1)} %copy-done.1, bf16[2,512,8192]{2,1,0:T(8,128)(2,1)} %all-gather.6.cloned.1.call-done), kind=kOutput, calls=%fused_computation | convolution fusion | flops 2147483648 | bytes 17039360 | tf_op jit(solution)/shard_map/dot_general | solution.py:18
  105.3 10.0 %convolution_add_fusion = f32[256,8192]{0,1:T(8,128)} fusion(f32[256,8192]{0,1:T(8,128)S(1)} %convolution_bitcast_fusion, bf16[2,512,8192]{2,1,0:T(8,128)(2,1)} %all-gather.6.cloned.1.call-done, bf16[64,256]{1,0:T(8,128)(2,1)S(1)} %collective-permute-done, bf16[448,256]{1,0:T(8,128)(2,1)S(1)} %slice.12), kind=kOutput, calls=%fused_computation.1 | convolution fusion | flops 2150105088 | bytes 25427968 | tf_op jit(solution)/shard_map/dot_general | solution.py:18
  115.3 0.1 convert_reduce_fusion
  115.4 62.3 %psum.49 = f32[512]{0:T(512)S(1)} all-reduce(f32[512]{0:T(512)S(1)} %convert_reduce_fusion), channel_id=1, replica_groups=mesh['wide'=32,'narrow'=4] {'wide'}, use_global_device_ids=true, to_apply=%region_2.0 | all-reduce | flops 512 | bytes 4096 | tf_op jit(solution)/shard_map/psum | solution.py:27
  177.7 0.2 fusion.5
  177.9 17.7 %reduce-scatter.2.cloned.1.call-done = f32[256,2048]{0,1:T(8,128)} async-done(((f32[256,8192]{0,1:T(8,128)}), f32[256,2048]{0,1:T(8,128)}) %reduce-scatter.2.cloned.1.call-update) | async-done | bytes 2097168 | tf_op jit(solution)/shard_map/reduce_scatter | solution.py:32
  195.6 2.0 reduce_sum.55
  197.6 6.5 %all-reduce = (f32[256]{0:T(256)S(1)}, f32[256]{0:T(256)S(1)}) all-reduce(f32[256]{0:T(256)S(1)} %reduce_sum.55, f32[256]{0:T(256)S(1)} %bitcast.35), channel_id=1, replica_groups=mesh['wide'=32,'narrow'=4] {'narrow'}, use_global_device_ids=true, to_apply=%region_5.0 | all-reduce | flops 512 | bytes 4096 | tf_op jit(solution)/shard_map/psum | solution.py:33
  204.2 27.0 %all-gather = f32[32,1,256]{2,1,0:T(1,128)S(1)} all-gather(f32[1,1,256]{2,1,0:T(1,128)S(1)} %bitcast.31), channel_id=1, replica_groups=mesh['wide'=32,'narrow'=4] {'wide'}, dimensions={0}, use_global_device_ids=true | all-gather | bytes 33792 | tf_op jit(solution)/shard_map/all_gather | solution.py:34
  231.2 23.6 %all-gather.1 = f32[32,1,256]{2,1,0:T(1,128)S(1)} all-gather(f32[1,1,256]{2,1,0:T(1,128)S(1)} %bitcast.36), channel_id=1, replica_groups=mesh['wide'=32,'narrow'=4] {'wide'}, dimensions={0}, use_global_device_ids=true | all-gather | bytes 33792 | tf_op jit(solution)/shard_map/all_gather | solution.py:40
  254.8 0.4 fusion
  255.1 6.9 %psum.52 = f32[256]{0:T(256)S(1)} all-reduce(f32[256]{0:T(256)S(1)} %fusion), channel_id=1, replica_groups=mesh['wide'=32,'narrow'=4] {'narrow'}, use_global_device_ids=true, to_apply=%region_7.0 | all-reduce | flops 256 | bytes 2048 | tf_op jit(solution)/shard_map/psum | solution.py:45
  262.0 24.1 %all-gather.2 = f32[32,1,256]{2,1,0:T(1,128)S(1)} all-gather(f32[1,1,256]{2,1,0:T(1,128)S(1)} %bitcast.33), channel_id=1, replica_groups=mesh['wide'=32,'narrow'=4] {'wide'}, dimensions={0}, use_global_device_ids=true | all-gather | bytes 33792 | tf_op jit(solution)/shard_map/all_gather | solution.py:40
  286.1 0.4 fusion.1
  286.5 6.6 %psum.53 = f32[256]{0:T(256)S(1)} all-reduce(f32[256]{0:T(256)S(1)} %fusion.1), channel_id=1, replica_groups=mesh['wide'=32,'narrow'=4] {'narrow'}, use_global_device_ids=true, to_apply=%region_9.0 | all-reduce | flops 256 | bytes 2048 | tf_op jit(solution)/shard_map/psum | solution.py:45
  293.0 25.6 %all-gather.3 = f32[32,1,256]{2,1,0:T(1,128)S(1)} all-gather(f32[1,1,256]{2,1,0:T(1,128)S(1)} %bitcast.32), channel_id=1, replica_groups=mesh['wide'=32,'narrow'=4] {'wide'}, dimensions={0}, use_global_device_ids=true | all-gather | bytes 33792 | tf_op jit(solution)/shard_map/all_gather | solution.py:40
  318.6 0.4 fusion.2
  319.0 6.9 %psum.54 = f32[256]{0:T(256)S(1)} all-reduce(f32[256]{0:T(256)S(1)} %fusion.2), channel_id=1, replica_groups=mesh['wide'=32,'narrow'=4] {'narrow'}, use_global_device_ids=true, to_apply=%region_11.0 | all-reduce | flops 256 | bytes 2048 | tf_op jit(solution)/shard_map/psum | solution.py:45
  325.9 0.6 reduce_sum.59
  326.5 64.8 %psum.55 = f32[]{:T(128)} all-reduce(f32[]{:T(128)} %reduce_sum.59), channel_id=1, replica_groups=mesh['wide'=32,'narrow'=4] {'wide'}, use_global_device_ids=true, to_apply=%region_13.0 | all-reduce | flops 1 | bytes 8 | tf_op jit(solution)/shard_map/psum | solution.py:47
  391.3 1.2 multiply_divide_fusion.1
  392.5 1.8 multiply_divide_fusion
  394.3 2.9 copy.6
  (12 shorter events, 0.1 us)
Async XLA Ops:
  7.2 92.3 %copy-start.1 = (bf16[512,256]{1,0:T(8,128)(2,1)S(1)}, bf16[512,256]{1,0:T(8,128)(2,1)}, u32[]{:S(2)}) copy-start(bf16[512,256]{1,0:T(8,128)(2,1)} %param.1) | copy-start | bytes 786436
  7.2 92.3 %all-gather.6.cloned.1.call-start = ((), (), s32[]{:S(2)}) async-start(), calls=%async_computation.1 | async-start | bytes 17301504 | tf_op jit(solution)/shard_map/all_gather | solution.py:30
  8.0 5.3 %collective-permute-start = (bf16[64,256]{1,0:T(8,128)(2,1)S(1)}, bf16[64,256]{1,0:T(8,128)(2,1)S(1)}, u32[]{:S(2)}, u32[]{:S(2)}) collective-permute-start(bf16[64,256]{1,0:T(8,128)(2,1)S(1)} %slice.13), channel_id=1, source_target_pairs={{1,0},{2,1},{3,2},{5,4},{6,5},{7,6},{9,8},{10,9},{11,10},{13,12},{... | collective-permute-start | bytes 98312 | tf_op jit(solution)/shard_map/ppermute | solution.py:14
  15.2 180.4 %reduce-scatter.2.cloned.1.call-start = ((), (), s32[]{:S(2)}) async-start(), calls=%async_computation.2 | async-start | bytes 10485760 | tf_op jit(solution)/shard_map/reduce_scatter | solution.py:32
  195.6 59.2 %copy-start = (f32[256,2048]{0,1:T(8,128)S(1)}, f32[256,2048]{0,1:T(8,128)}, u32[]{:S(2)}) copy-start(f32[256,2048]{0,1:T(8,128)} %reduce-scatter.2.cloned.1.call-done) | copy-start | bytes 6291460
Sparse Core Ops, SparseCore 0:
  15.3 84.1 all-gather.5
  115.4 80.1 reduce-scatter.1
where the time goes:
time: 405 us; the launch traced here: 404 us
  blocking collectives  254 us (63%)
  waiting for transfers between devices  105 us (26%)
  matrix products  15.9 us (4%)
  between operations  14.1 us (3%)
  other arithmetic  8.7 us (2%)
  local copies, waits for them, and re-layouts  4.64 us (1%)
    all_gather x1, waiting for transfers between devices, shards(): piece = lax.all_gather(stacked, 'wide', axis=2, tiled=True)  84.3 us
    all_gather x3, blocking collectives, shards(): all_rows = lax.all_gather(row_now, 'wide', axis=0, tiled=True)  73.2 us
    psum x1, blocking collectives, shards(): grand = lax.psum(jnp.sum(row_now), 'wide')  64.8 us
    psum x1, blocking collectives, shards(): frame_totals = lax.psum(frame_part, 'wide')  62.3 us
    all_gather x1, blocking collectives, shards(): visit_all = lax.all_gather(visit_rows, 'wide', axis=0, tiled=True)  27 us
    psum x3, blocking collectives, shards(): row_now = lax.psum(jnp.sum(estimate, axis=1), 'narrow')  20.3 us
    reduce_scatter x1, waiting for transfers between devices, shards(): lax.psum_scatter(partial_value, 'narrow', scatter_dimension=1, tiled=True)  17.7 us
    dot_general x2, matrix products, contract_frames(): lax.dot_general(left, right, (((0,), (0,)), ((), ())), preferred_element_...  15.7 us
  transfers between devices with their start and end apart: 3, of which 3 were waited for; matrix products, arithmetic and copies ran while one was open for 0% of the time, Pallas kernels for 0%

commit v1 on v0

--- a/solution.py
+++ b/solution.py
@@ -31,7 +31,9 @@
     partial_value = contract_frames(member, piece[1]) + contract_frames(lagged, piece[0])
     counts = lax.psum_scatter(partial_value, "narrow", scatter_dimension=1, tiled=True)
     row_now, visit_rows = lax.psum((jnp.sum(counts, axis=1), visit_part), "narrow")
-    visit_all = lax.all_gather(visit_rows, "wide", axis=0, tiled=True)
+    visit_all = jnp.concatenate(
+        lax.all_to_all(jnp.stack([visit_rows] * lax.axis_size("wide")), "wide", 0, 0), axis=0
+    )
     width_cols = counts.shape[1]
     col_start = lax.axis_index("narrow") * width_cols
     visit_cols = lax.dynamic_slice_in_dim(visit_all, col_start, width_cols)

time: 405 us -> 389 us (0.960)
  blocking collectives: 254 us -> 228 us
  starting transfers between devices: 1.36 us -> 11.1 us
    all_gather x1 -> x0, blocking collectives: 27 us -> none  [shards(): visit_all = lax.all_gather(visit_rows, 'wide', axis=0, tiled=True)]
    all_to_all x0 -> x1, starting transfers between devices: none -> 9.74 us  [shards(): lax.all_to_all(jnp.stack([visit_rows] * lax.axis_size('wide')), 'wide', 0...]
  transfers between devices with their start and end apart: 3 -> 4, of which waited for: 3 -> 3; matrix products, arithmetic and copies ran while one was open for 0% -> 0% of each run, Pallas kernels for 0% -> 0%
where the time goes in v1:
time: 389 us; the launch traced here: 388 us
  blocking collectives  228 us (59%)
  waiting for transfers between devices  105 us (27%)
  matrix products  15.9 us (4%)
  between operations  14.1 us (4%)
  starting transfers between devices  11.1 us (3%)
  other arithmetic  8.7 us (2%)
  local copies, waits for them, and re-layouts  5.28 us (1%)
    all_gather x1, waiting for transfers between devices, shards(): piece = lax.all_gather(stacked, 'wide', axis=2, tiled=True)  84.3 us
    all_gather x3, blocking collectives, shards(): all_rows = lax.all_gather(row_now, 'wide', axis=0, tiled=True)  74.3 us
    psum x1, blocking collectives, shards(): grand = lax.psum(jnp.sum(row_now), 'wide')  64.8 us
    psum x1, blocking collectives, shards(): frame_totals = lax.psum(frame_part, 'wide')  62.3 us
    psum x3, blocking collectives, shards(): row_now = lax.psum(jnp.sum(estimate, axis=1), 'narrow')  20.4 us
    reduce_scatter x1, waiting for transfers between devices, shards(): lax.psum_scatter(partial_value, 'narrow', scatter_dimension=1, tiled=True)  17.7 us
    dot_general x2, matrix products, contract_frames(): lax.dot_general(left, right, (((0,), (0,)), ((), ())), preferred_element_...  15.7 us
    all_to_all x1, starting transfers between devices, shards(): lax.all_to_all(jnp.stack([visit_rows] * lax.axis_size('wide')), 'wide', 0...  9.74 us
  transfers between devices with their start and end apart: 4, of which 3 were waited for; matrix products, arithmetic and copies ran while one was open for 0% of the time, Pallas kernels for 0%

profile of v1, /device:TPU:1, one launch (start us, length us, event | category | flops | bytes accessed | tf_op | source)
XLA Modules:
  0.0 388.5 jit_solution(3196518839189607367)
XLA Ops:
  7.2 0.0 all-gather.5.cloned.1.call-start
  7.2 0.8 slice.13
  8.0 1.3 collective-permute-start
  9.3 1.0 slice.12
  10.3 3.1 collective-permute-done
  13.3 1.8 pad_maximum_fusion
  15.2 0.0 reduce-scatter.2.cloned.1.call-start
  15.2 84.3 %all-gather.5.cloned.1.call-done = bf16[2,512,8192]{2,1,0:T(8,128)(2,1)} async-done(((bf16[2,512,256]{2,1,0:T(8,128)(2,1)}), bf16[2,512,8192]{2,1,0:T(8,128)(2,1)}) %all-gather.5.cloned.1.call-update) | async-done | bytes 16777232 | tf_op jit(solution)/shard_map/all_gather | solution.py:30
  99.5 5.8 %convolution_bitcast_fusion = f32[256,8192]{0,1:T(8,128)S(1)} fusion(bf16[512,256]{1,0:T(8,128)(2,1)S(1)} %copy-done.1, bf16[2,512,8192]{2,1,0:T(8,128)(2,1)} %all-gather.5.cloned.1.call-done), kind=kOutput, calls=%fused_computation | convolution fusion | flops 2147483648 | bytes 17039360 | tf_op jit(solution)/shard_map/dot_general | solution.py:18
  105.3 10.0 %convolution_add_fusion = f32[256,8192]{0,1:T(8,128)} fusion(f32[256,8192]{0,1:T(8,128)S(1)} %convolution_bitcast_fusion, bf16[2,512,8192]{2,1,0:T(8,128)(2,1)} %all-gather.5.cloned.1.call-done, bf16[64,256]{1,0:T(8,128)(2,1)S(1)} %collective-permute-done, bf16[448,256]{1,0:T(8,128)(2,1)S(1)} %slice.12), kind=kOutput, calls=%fused_computation.1 | convolution fusion | flops 2150105088 | bytes 25427968 | tf_op jit(solution)/shard_map/dot_general | solution.py:18
  115.3 0.1 convert_reduce_fusion
  115.4 62.3 %psum.49 = f32[512]{0:T(512)S(1)} all-reduce(f32[512]{0:T(512)S(1)} %convert_reduce_fusion), channel_id=1, replica_groups=mesh['wide'=32,'narrow'=4] {'wide'}, use_global_device_ids=true, to_apply=%region_2.0 | all-reduce | flops 512 | bytes 4096 | tf_op jit(solution)/shard_map/psum | solution.py:27
  177.7 0.2 fusion.5
  177.9 17.7 %reduce-scatter.2.cloned.1.call-done = f32[256,2048]{0,1:T(8,128)} async-done(((f32[256,8192]{0,1:T(8,128)}), f32[256,2048]{0,1:T(8,128)}) %reduce-scatter.2.cloned.1.call-update) | async-done | bytes 2097168 | tf_op jit(solution)/shard_map/reduce_scatter | solution.py:32
  195.6 2.0 reduce_sum.55
  197.6 6.5 %all-reduce = (f32[256]{0:T(256)S(1)}, f32[256]{0:T(256)S(1)}) all-reduce(f32[256]{0:T(256)S(1)} %reduce_sum.55, f32[256]{0:T(256)S(1)} %bitcast.33), channel_id=1, replica_groups=mesh['wide'=32,'narrow'=4] {'narrow'}, use_global_device_ids=true, to_apply=%region_5.0 | all-reduce | flops 512 | bytes 4096 | tf_op jit(solution)/shard_map/psum | solution.py:33
  204.2 0.6 stack.11
  204.8 9.7 %all-to-all-start = ((f32[32,1,256]{2,1,0:T(1,128)}), f32[32,1,256]{2,1,0:T(1,128)S(1)}, u32[]{:S(2)}, u32[]{:S(2)}) async-start(f32[32,1,256]{2,1,0:T(1,128)} %stack.11), calls=%async_computation.1 | async-start | bytes 65536 | tf_op jit(solution)/shard_map/all_to_all | solution.py:35
  214.6 24.6 %all-gather = f32[32,1,256]{2,1,0:T(1,128)S(1)} all-gather(f32[1,1,256]{2,1,0:T(1,128)S(1)} %bitcast.34), channel_id=1, replica_groups=mesh['wide'=32,'narrow'=4] {'wide'}, dimensions={0}, use_global_device_ids=true | all-gather | bytes 33792 | tf_op jit(solution)/shard_map/all_gather | solution.py:42
  239.2 0.4 fusion
  239.6 6.9 %psum.52 = f32[256]{0:T(256)S(1)} all-reduce(f32[256]{0:T(256)S(1)} %fusion), channel_id=1, replica_groups=mesh['wide'=32,'narrow'=4] {'narrow'}, use_global_device_ids=true, to_apply=%region_7.0 | all-reduce | flops 256 | bytes 2048 | tf_op jit(solution)/shard_map/psum | solution.py:47
  246.5 25.6 %all-gather.1 = f32[32,1,256]{2,1,0:T(1,128)S(1)} all-gather(f32[1,1,256]{2,1,0:T(1,128)S(1)} %bitcast.31), channel_id=1, replica_groups=mesh['wide'=32,'narrow'=4] {'wide'}, dimensions={0}, use_global_device_ids=true | all-gather | bytes 33792 | tf_op jit(solution)/shard_map/all_gather | solution.py:42
  272.1 0.4 fusion.1
  272.5 6.6 %psum.53 = f32[256]{0:T(256)S(1)} all-reduce(f32[256]{0:T(256)S(1)} %fusion.1), channel_id=1, replica_groups=mesh['wide'=32,'narrow'=4] {'narrow'}, use_global_device_ids=true, to_apply=%region_9.0 | all-reduce | flops 256 | bytes 2048 | tf_op jit(solution)/shard_map/psum | solution.py:47
  279.0 24.0 %all-gather.2 = f32[32,1,256]{2,1,0:T(1,128)S(1)} all-gather(f32[1,1,256]{2,1,0:T(1,128)S(1)} %bitcast.30), channel_id=1, replica_groups=mesh['wide'=32,'narrow'=4] {'wide'}, dimensions={0}, use_global_device_ids=true | all-gather | bytes 33792 | tf_op jit(solution)/shard_map/all_gather | solution.py:42
  303.1 0.4 fusion.2
  303.5 6.9 %psum.54 = f32[256]{0:T(256)S(1)} all-reduce(f32[256]{0:T(256)S(1)} %fusion.2), channel_id=1, replica_groups=mesh['wide'=32,'narrow'=4] {'narrow'}, use_global_device_ids=true, to_apply=%region_11.0 | all-reduce | flops 256 | bytes 2048 | tf_op jit(solution)/shard_map/psum | solution.py:47
  310.4 0.6 reduce_sum.59
  311.0 64.8 %psum.55 = f32[]{:T(128)} all-reduce(f32[]{:T(128)} %reduce_sum.59), channel_id=1, replica_groups=mesh['wide'=32,'narrow'=4] {'wide'}, use_global_device_ids=true, to_apply=%region_13.0 | all-reduce | flops 1 | bytes 8 | tf_op jit(solution)/shard_map/psum | solution.py:49
  375.8 1.2 multiply_divide_fusion.1
  377.0 1.8 multiply_divide_fusion
  378.8 2.9 copy.6
  (14 shorter events, 0.1 us)
Async XLA Ops:
  7.2 92.3 %copy-start.1 = (bf16[512,256]{1,0:T(8,128)(2,1)S(1)}, bf16[512,256]{1,0:T(8,128)(2,1)}, u32[]{:S(2)}) copy-start(bf16[512,256]{1,0:T(8,128)(2,1)} %param.1) | copy-start | bytes 786436
  7.2 92.3 %all-gather.5.cloned.1.call-start = ((), (), s32[]{:S(2)}) async-start(), calls=%async_computation.2 | async-start | bytes 17301504 | tf_op jit(solution)/shard_map/all_gather | solution.py:30
  8.0 5.3 %collective-permute-start = (bf16[64,256]{1,0:T(8,128)(2,1)S(1)}, bf16[64,256]{1,0:T(8,128)(2,1)S(1)}, u32[]{:S(2)}, u32[]{:S(2)}) collective-permute-start(bf16[64,256]{1,0:T(8,128)(2,1)S(1)} %slice.13), channel_id=1, source_target_pairs={{1,0},{2,1},{3,2},{5,4},{6,5},{7,6},{9,8},{10,9},{11,10},{13,12},{... | collective-permute-start | bytes 98312 | tf_op jit(solution)/shard_map/ppermute | solution.py:14
  15.2 180.4 %reduce-scatter.2.cloned.1.call-start = ((), (), s32[]{:S(2)}) async-start(), calls=%async_computation.3 | async-start | bytes 10485760 | tf_op jit(solution)/shard_map/reduce_scatter | solution.py:32
  195.6 43.6 %copy-start = (f32[256,2048]{0,1:T(8,128)S(1)}, f32[256,2048]{0,1:T(8,128)}, u32[]{:S(2)}) copy-start(f32[256,2048]{0,1:T(8,128)} %reduce-scatter.2.cloned.1.call-done) | copy-start | bytes 6291460
  204.8 34.4 %all-to-all-start = ((f32[32,1,256]{2,1,0:T(1,128)}), f32[32,1,256]{2,1,0:T(1,128)S(1)}, u32[]{:S(2)}, u32[]{:S(2)}) async-start(f32[32,1,256]{2,1,0:T(1,128)} %stack.11), calls=%async_computation.1 | async-start | bytes 65536 | tf_op jit(solution)/shard_map/all_to_all | solution.py:35
Sparse Core Ops, SparseCore 0:
  15.3 84.1 all-gather.4
  115.4 80.1 reduce-scatter.1
